TPU v7x, 128 devices: a whole 4x4x4 slice. The times are simulated.
128 devices in a mesh: sx: 8 (over y, z_lo), sz: 16 (over x, z_hi, core).
Axes of the slice: x: 4, y: 4, z: 4 (z_hi: 2, z_lo: 2; z = z_hi * 2 + z_lo), core: 2. Of those that a mesh axis runs over, the one named last changes fastest.
Arguments:
- right_side: float32 [72, 256, 4096], P('sx', 'sz'), may hold values from -6 to 6
- coupling: bfloat16 [72, 5, 256, 256], P('sx'), may hold values from -0.15625 to 0.15625
- harmonic_offsets: int32 [5], replicated, may hold values from -6 to 6, as said below
- eigen_basis: bfloat16 [256, 256], replicated, may hold values from -0.375 to 0.375
- eigen_inverse: bfloat16 [256, 256], replicated, may hold values from -0.375 to 0.375
- eigen_size: float32 [256], replicated, may hold values from 0.5 to 50
Outputs:
- solution: float32 [72, 256, 4096], P('sx', 'sz')
Inputs may be any that keep to these rules, and one draw needn't show every extreme that they name: `harmonic_offsets`: the offsets are distinct; some offset equals 6 and some equals -6.
All inputs are finite; a program needn't handle non-finite values.
Results may differ from a plain program's by a relative error of at most 0.00065.
The roundings to bfloat16 on the way count: a program that leaves them out, or rounds other values in their place, can miss the bound.
Values may be sent and summed in bfloat16 or wider, within the bound.
A program may use at most 128 MiB of HBM per device.

v0:
```python
import jax
import jax.numpy as jnp
from jax import lax
from jax.sharding import PartitionSpec as P

KX = 72
KZ = 128
H = 5
OFF = 6
STEPS = 2
R = 32


def extended(value, sides, width):
    for axis, dim in sides:
        peers, length = (lax.axis_size(axis), value.shape[dim])
        up = [(i, (i + 1) % peers) for i in range(peers)]
        down = [(j, i) for i, j in up]
        last = lax.slice_in_dim(value, length - width, length, axis=dim)
        first = lax.slice_in_dim(value, 0, width, axis=dim)
        before = lax.ppermute(last, axis, up)
        after = lax.ppermute(first, axis, down)
        value = jnp.concatenate([before, value, after], axis=dim)
    return value


def wave_table(mode_count, span_count):
    first_mode = lax.axis_index("sx") * mode_count
    first_span = lax.axis_index("sz") * span_count
    modes = first_mode + jnp.arange(mode_count, dtype=jnp.int32)
    spans = first_span + jnp.arange(span_count, dtype=jnp.int32)
    signed_x = jnp.where(modes < KX // 2, modes, modes - KX).astype(jnp.float32) * (4.0 / KX)
    signed_z = jnp.where(spans < KZ // 2, spans, spans - KZ).astype(jnp.float32) * (4.0 / KZ)
    table = 1.0 + signed_x[:, None] ** 2 + signed_z[None, :] ** 2
    return jnp.repeat(table, R, axis=1)


def precondition(residual, eigen_basis, eigen_inverse, eigen_size, wave_square):
    rounded = residual.astype(jnp.bfloat16)
    spectral = jnp.einsum("ij,kjc->kic", eigen_inverse, rounded, preferred_element_type=jnp.float32)
    factor = -1.0 / (eigen_size[None, :, None] + wave_square[:, None, :])
    scaled = (spectral * factor).astype(jnp.bfloat16)
    result = jnp.einsum("ij,kjc->kic", eigen_basis, scaled, preferred_element_type=jnp.float32)
    return result.astype(jnp.bfloat16)


def apply_operator(search, coupling, harmonic_offsets, wave_square):
    mode_count = search.shape[0]
    padded = extended(search, (("sx", 0),), OFF)
    accum = -wave_square[:, None, :] * search.astype(jnp.float32)
    for harmonic in range(H):
        source = lax.dynamic_slice_in_dim(padded, OFF + harmonic_offsets[harmonic], mode_count, 0)
        accum = accum + jnp.einsum(
            "kij,kjc->kic", coupling[:, harmonic], source, preferred_element_type=jnp.float32
        )
    return accum


def relax(solution, residual, search_full, image):
    inner = jnp.sum(jnp.sum(image * residual, axis=(0, 1)).reshape(-1, R), axis=0)
    energy = jnp.sum(jnp.sum(image * image, axis=(0, 1)).reshape(-1, R), axis=0)
    aligned, total_energy = lax.psum((inner, energy), ("sx", "sz"))
    step_size = jnp.tile(aligned / (total_energy + 1e-06), image.shape[2] // R)
    return (solution + step_size * search_full, residual - step_size * image)


def shards(right_side, coupling, harmonic_offsets, eigen_basis, eigen_inverse, eigen_size):
    residual = lax.all_to_all(right_side, "sz", split_axis=2, concat_axis=1, tiled=True)
    wave_square = wave_table(residual.shape[0], residual.shape[2] // R)
    solution = jnp.zeros_like(residual)
    for sweep in range(STEPS):
        search = precondition(residual, eigen_basis, eigen_inverse, eigen_size, wave_square)
        image = apply_operator(search, coupling, harmonic_offsets, wave_square)
        solution, residual = relax(solution, residual, search.astype(jnp.float32), image)
    return lax.all_to_all(solution, "sz", split_axis=1, concat_axis=2, tiled=True)


def solution(mesh):
    in_specs = (P("sx", "sz", None), P("sx", None, None, None), P(), P(), P(), P())
    out_specs = P("sx", "sz", None)
    return jax.shard_map(shards, mesh=mesh, in_specs=in_specs, out_specs=out_specs, check_vma=False)
```

profile of v0, /device:TPU:1, one launch (start us, length us, event | category | flops | bytes accessed | tf_op | source)
XLA Modules:
  0.0 424.5 jit_solution(962264210277215487)
XLA Ops:
  0.0 0.0 copy-start
  0.0 17.6 %copy.68 = f32[9,16,4096]{1,0,2:T(8,128)} copy(f32[9,16,4096]{2,1,0:T(8,128)} %param.6) | data formatting | bytes 4718592 | tf_op args[0]
  17.6 19.3 %reshape.75 = f32[16,1,36864]{2,1,0:T(1,128)} reshape(f32[4096,9,16]{2,1,0:T(8,128)} %bitcast.113) | data formatting | bytes 4718592
  36.9 9.1 %all-to-all-start = ((f32[16,1,36864]{2,1,0:T(1,128)}), f32[16,1,36864]{2,1,0:T(1,128)S(1)}, u32[]{:S(2)}, u32[]{:S(2)}) async-start(f32[16,1,36864]{2,1,0:T(1,128)} %reshape.75), calls=%async_computation | async-start | bytes 4718592 | tf_op jit(solution)/shard_map/all_to_all | solution.py:68
  46.1 0.1 broadcast_add_fusion
  46.1 0.1 broadcast_in_dim.2
  46.2 0.1 broadcast_in_dim_reshape.2
  46.3 31.0 %all-to-all-done = f32[16,1,36864]{2,1,0:T(1,128)S(1)} async-done(((f32[16,1,36864]{2,1,0:T(1,128)}), f32[16,1,36864]{2,1,0:T(1,128)S(1)}, u32[]{:S(2)}, u32[]{:S(2)}) %all-to-all-start) | async-done | bytes 2359328 | tf_op jit(solution)/shard_map/all_to_all | solution.py:68
  77.3 1.4 copy-done.4
  78.7 0.6 broadcast.95
  79.3 8.0 %reduce = f32[16,36864]{1,0:T(8,128)S(1)} reduce(f32[16,1,36864]{2,1,0:T(1,128)} %copy-done.4, f32[]{:T(128)} %broadcast.95), dimensions={1}, to_apply=%all_to_all.26.reduce_sub_computation | reduce | bytes 4718596 | tf_op jit(solution)/shard_map/all_to_all | solution.py:68
  87.3 21.2 %reshape.76 = f32[4096,9,16]{2,1,0:T(8,128)} reshape(f32[16,36864]{1,0:T(8,128)S(1)} %reduce) | data formatting | bytes 4718592
  108.5 18.9 %copy.70 = f32[9,16,16,256]{3,2,1,0:T(8,128)S(1)} copy(f32[9,16,16,256]{2,0,3,1:T(8,128)} %bitcast.112) | data formatting | bytes 4718592 | tf_op jit(solution)/shard_map/all_to_all | solution.py:68
  127.4 0.0 copy-start.7
  127.4 1.5 copy.71
  128.9 0.0 copy-done
  128.9 0.0 copy-done.6
  128.9 3.3 fusion.13
  132.2 2.4 fusion.89
  134.6 0.7 collective-permute-start
  135.3 2.8 collective-permute-start.1
  138.1 0.7 fusion.90
  145.0 23.4 %collective-permute-done = bf16[6,256,256]{2,1,0:T(8,128)(2,1)} collective-permute-done((bf16[6,256,256]{2,1,0:T(8,128)(2,1)}, bf16[6,256,256]{2,1,0:T(8,128)(2,1)}, u32[]{:S(2)}, u32[]{:S(2)}) %collective-permute-start) | collective-permute-done | bytes 786464 | tf_op jit(solution)/shard_map/ppermute | solution.py:21
  168.4 2.3 collective-permute-done.1
  170.7 2.2 pad_maximum_fusion
  172.9 0.0 slice-start.1
  172.9 1.9 fusion.21
  174.8 1.8 fusion.25
  176.5 0.0 slice-done
  176.5 0.0 slice-done.1
  176.6 0.5 fusion.29
  177.0 0.0 copy-start.1
  177.0 0.5 fusion.17
  177.5 0.8 copy-done.1
  178.3 2.7 multiply_reduce_fusion.2
  181.0 0.1 reshape.69
  181.1 0.1 reshape.70
  181.2 67.8 %all-reduce.1 = (f32[32]{0:T(128)S(1)}, f32[32]{0:T(128)S(1)}) all-reduce(f32[32]{0:T(128)S(1)} %reduce_sum.73, f32[32]{0:T(128)S(1)} %reduce_sum.75), channel_id=1, replica_groups=mesh['sx'=8,'sz'=16] {'sx','sz'}, use_global_device_ids=true, to_apply=%region_2.3 | all-reduce | flops 64 | bytes 512 | tf_op jit(solution)/shard_map/psum | solution.py:62
  249.0 0.1 mul.87
  249.1 3.8 fusion.14
  252.9 1.6 fusion.88
  254.5 0.3 collective-permute-start.2
  254.8 3.3 collective-permute-start.3
  258.2 29.7 %collective-permute-done.2 = bf16[6,256,256]{2,1,0:T(8,128)(2,1)S(1)} collective-permute-done((bf16[6,256,256]{2,1,0:T(8,128)(2,1)S(1)}, bf16[6,256,256]{2,1,0:T(8,128)(2,1)S(1)}, u32[]{:S(2)}, u32[]{:S(2)}) %collective-permute-start.2) | collective-permute-done | bytes 786464 | tf_op jit(solution)/shard_map/ppermute | solution.py:21
  287.9 1.9 collective-permute-done.3
  289.8 1.6 pad_maximum_fusion.1
  291.4 1.8 fusion.23
  293.2 0.5 fusion.27
  293.7 0.5 fusion.31
  294.1 0.0 copy-start.2
  294.1 0.0 copy-start.3
  294.2 0.5 fusion.19
  294.6 0.8 copy-done.2
  295.4 0.8 copy-done.3
  296.2 1.5 multiply_reduce_fusion
  297.7 0.1 reshape.71
  297.8 0.1 reshape.72
  297.9 65.3 %all-reduce = (f32[32]{0:T(128)S(1)}, f32[32]{0:T(128)S(1)}) all-reduce(f32[32]{0:T(128)S(1)} %reduce_sum.77, f32[32]{0:T(128)S(1)} %reduce_sum.79), channel_id=1, replica_groups=mesh['sx'=8,'sz'=16] {'sx','sz'}, use_global_device_ids=true, to_apply=%region_8.9 | all-reduce | flops 64 | bytes 512 | tf_op jit(solution)/shard_map/psum | solution.py:62
  363.2 0.1 mul.95
  363.3 2.0 fusion.5
  365.3 1.5 copy.80
  366.8 54.6 %all_to_all.36 = f32[9,256,256]{2,0,1:T(8,128)S(1)} all-to-all(f32[9,256,256]{2,0,1:T(8,128)S(1)} %copy.80), channel_id=1, replica_groups=mesh['sx'=8,'sz'=16] {'sz'}, dimensions={1} | all-to-all | bytes 4718592 | tf_op jit(solution)/shard_map/all_to_all | solution.py:75
  421.5 1.4 copy.81
  422.8 1.6 all_to_all.33
  (23 shorter events, 0.1 us)
Async XLA Ops:
  0.0 128.9 %copy-start = (bf16[256,256]{1,0:T(8,128)(2,1)S(1)}, bf16[256,256]{1,0:T(8,128)(2,1)}, u32[]{:S(2)}) copy-start(bf16[256,256]{1,0:T(8,128)(2,1)} %param.9) | copy-start | bytes 393220
  36.9 40.4 %all-to-all-start = ((f32[16,1,36864]{2,1,0:T(1,128)}), f32[16,1,36864]{2,1,0:T(1,128)S(1)}, u32[]{:S(2)}, u32[]{:S(2)}) async-start(f32[16,1,36864]{2,1,0:T(1,128)} %reshape.75), calls=%async_computation | async-start | bytes 4718592 | tf_op jit(solution)/shard_map/all_to_all | solution.py:68
  77.3 1.4 copy-start.4
  127.4 1.5 copy-start.6
  127.4 1.5 copy-start.7
  132.2 5.9 %copy-start.5 = (s32[5]{0:T(128)S(1)}, s32[5]{0:T(128)}, u32[]{:S(2)}) copy-start(s32[5]{0:T(128)} %param.8) | copy-start | bytes 64
  134.6 33.8 %collective-permute-start = (bf16[6,256,256]{2,1,0:T(8,128)(2,1)}, bf16[6,256,256]{2,1,0:T(8,128)(2,1)}, u32[]{:S(2)}, u32[]{:S(2)}) collective-permute-start(bf16[6,256,256]{2,1,0:T(8,128)(2,1)} %get-tuple-element.15), channel_id=1, source_target_pairs={{0,16},{16,32},{32,48},{48,64},{64,80},{80,96},{96,112},{112,0},{1... | collective-permute-start | bytes 2359304 | tf_op jit(solution)/shard_map/ppermute | solution.py:21
  135.3 35.4 %collective-permute-start.1 = (bf16[6,256,256]{2,1,0:T(8,128)(2,1)S(1)}, bf16[6,256,256]{2,1,0:T(8,128)(2,1)}, u32[]{:S(2)}, u32[]{:S(2)}) collective-permute-start(bf16[6,256,256]{2,1,0:T(8,128)(2,1)S(1)} %get-tuple-element.16), channel_id=1, source_target_pairs={{16,0},{32,16},{48,32},{64,48},{80,64},{96,80},{112,96},{0,112},{1... | collective-permute-start | bytes 2359304 | tf_op jit(solution)/shard_map/ppermute | solution.py:22
  170.7 5.9 %slice-start = ((s8[5898240]{0:T(1024)(128)(4,1)}), s8[4194304]{0:T(1024)(128)(4,1)S(1)}, s32[]{:S(2)}) async-start(s8[5898240]{0:T(1024)(128)(4,1)} %bitcast.116), calls=%async_computation.2 | async-start | bytes 8388608
  172.9 3.7 slice-start.1
  177.0 1.3 copy-start.1
  252.9 40.3 %slice-start.2 = ((s8[5898240]{0:T(1024)(128)(4,1)}), s8[4194304]{0:T(1024)(128)(4,1)S(1)}, s32[]{:S(2)}) async-start(s8[5898240]{0:T(1024)(128)(4,1)} %bitcast.118), calls=%async_computation.4 | async-start | bytes 8388608
  254.5 33.4 %collective-permute-start.2 = (bf16[6,256,256]{2,1,0:T(8,128)(2,1)S(1)}, bf16[6,256,256]{2,1,0:T(8,128)(2,1)S(1)}, u32[]{:S(2)}, u32[]{:S(2)}) collective-permute-start(bf16[6,256,256]{2,1,0:T(8,128)(2,1)S(1)} %get-tuple-element.13), channel_id=1, source_target_pairs={{0,16},{16,32},{32,48},{48,64},{64,80},{80,96},{96,112},{112,0},{1... | collective-permute-start | bytes 2359304 | tf_op jit(solution)/shard_map/ppermute | solution.py:21
  254.8 38.3 %slice-start.3 = ((s8[5898240]{0:T(1024)(128)(4,1)}), s8[1703936]{0:T(1024)(128)(4,1)S(1)}, s32[]{:S(2)}) async-start(s8[5898240]{0:T(1024)(128)(4,1)} %bitcast.118), calls=%async_computation.5 | async-start | bytes 3407872
  254.8 35.0 %collective-permute-start.3 = (bf16[6,256,256]{2,1,0:T(8,128)(2,1)S(1)}, bf16[6,256,256]{2,1,0:T(8,128)(2,1)S(1)}, u32[]{:S(2)}, u32[]{:S(2)}) collective-permute-start(bf16[6,256,256]{2,1,0:T(8,128)(2,1)S(1)} %get-tuple-element.14), channel_id=1, source_target_pairs={{16,0},{32,16},{48,32},{64,48},{80,64},{96,80},{112,96},{0,112},{1... | collective-permute-start | bytes 2359304 | tf_op jit(solution)/shard_map/ppermute | solution.py:22
  294.1 1.3 copy-start.2
  294.1 2.0 copy-start.3
where the time goes:
time: 426 us; the launch traced here: 424 us
  blocking collectives  188 us (44%)
  local copies, waits for them, and re-layouts  92.6 us (22%)
  waiting for transfers between devices  88.3 us (21%)
  matrix products  19.1 us (4%)
  starting transfers between devices  16.3 us (4%)
  other arithmetic  13.9 us (3%)
  between operations  6.39 us (2%)
    psum x2, blocking collectives, relax(): aligned, total_energy = lax.psum((inner, energy), ('sx', 'sz'))  133 us
    unnamed x27, local copies, waits for them, and re-layouts  61.9 us
    all_to_all x1, blocking collectives, shards(): lax.all_to_all(solution, 'sz', split_axis=1, concat_axis=2, tiled=True)  54.6 us
    ppermute x2, waiting for transfers between devices, extended(): before = lax.ppermute(last, axis, up)  53.1 us
    all_to_all x1, waiting for transfers between devices, shards(): lax.all_to_all(right_side, 'sz', split_axis=2, concat_axis=1, tiled=True)  31 us
    all_to_all x3, local copies, waits for them, and re-layouts, shards(): lax.all_to_all(right_side, 'sz', split_axis=2, concat_axis=1, tiled=True)  21 us
    dot_general x10, matrix products, apply_operator(): jnp.einsum('kij,kjc->kic', coupling[:, harmonic], source, preferred_eleme...  12 us
    all_to_all x1, starting transfers between devices, shards(): lax.all_to_all(right_side, 'sz', split_axis=2, concat_axis=1, tiled=True)  9.13 us
  transfers between devices with their start and end apart: 5, of which 5 were waited for; matrix products, arithmetic and copies ran while one was open for 0% of the time, Pallas kernels for 0%

commit v1 on v0

--- a/solution.py
+++ b/solution.py
@@ -59,7 +59,7 @@
 def relax(solution, residual, search_full, image):
     inner = jnp.sum(jnp.sum(image * residual, axis=(0, 1)).reshape(-1, R), axis=0)
     energy = jnp.sum(jnp.sum(image * image, axis=(0, 1)).reshape(-1, R), axis=0)
-    aligned, total_energy = lax.psum((inner, energy), ("sx", "sz"))
+    aligned, total_energy = lax.psum(lax.psum((inner, energy), "sx"), "sz")
     step_size = jnp.tile(aligned / (total_energy + 1e-06), image.shape[2] // R)
     return (solution + step_size * search_full, residual - step_size * image)
 

time: 426 us -> 395 us (0.927)
  blocking collectives: 188 us -> 157 us
    psum x2 -> x4, blocking collectives: 133 us -> 103 us  [relax(): aligned, total_energy = lax.psum(lax.psum((inner, energy), 'sx'), 'sz')]
where the time goes in v1:
time: 395 us; the launch traced here: 394 us
  blocking collectives  157 us (40%)
  local copies, waits for them, and re-layouts  92.7 us (23%)
  waiting for transfers between devices  88.5 us (22%)
  matrix products  19.1 us (5%)
  starting transfers between devices  16.3 us (4%)
  other arithmetic  13.9 us (4%)
  between operations  6.4 us (2%)
    psum x4, blocking collectives, relax(): aligned, total_energy = lax.psum(lax.psum((inner, energy), 'sx'), 'sz')  103 us
    unnamed x27, local copies, waits for them, and re-layouts  61.9 us
    all_to_all x1, blocking collectives, shards(): lax.all_to_all(solution, 'sz', split_axis=1, concat_axis=2, tiled=True)  53.9 us
    ppermute x2, waiting for transfers between devices, extended(): before = lax.ppermute(last, axis, up)  53.2 us
    all_to_all x1, waiting for transfers between devices, shards(): lax.all_to_all(right_side, 'sz', split_axis=2, concat_axis=1, tiled=True)  31 us
    all_to_all x3, local copies, waits for them, and re-layouts, shards(): lax.all_to_all(right_side, 'sz', split_axis=2, concat_axis=1, tiled=True)  21 us
    dot_general x10, matrix products, apply_operator(): jnp.einsum('kij,kjc->kic', coupling[:, harmonic], source, preferred_eleme...  12 us
    all_to_all x1, starting transfers between devices, shards(): lax.all_to_all(right_side, 'sz', split_axis=2, concat_axis=1, tiled=True)  9.13 us
  transfers between devices with their start and end apart: 5, of which 5 were waited for; matrix products, arithmetic and copies ran while one was open for 0% of the time, Pallas kernels for 0%

profile of v1, /device:TPU:1, one launch (start us, length us, event | category | flops | bytes accessed | tf_op | source)
XLA Modules:
  0.0 393.9 jit_solution(7576631855805190157)
XLA Ops:
  0.0 0.0 copy-start
  0.0 17.6 %copy.68 = f32[9,16,4096]{1,0,2:T(8,128)} copy(f32[9,16,4096]{2,1,0:T(8,128)} %param.6) | data formatting | bytes 4718592 | tf_op args[0]
  17.6 19.3 %reshape.75 = f32[16,1,36864]{2,1,0:T(1,128)} reshape(f32[4096,9,16]{2,1,0:T(8,128)} %bitcast.113) | data formatting | bytes 4718592
  36.9 9.1 %all-to-all-start = ((f32[16,1,36864]{2,1,0:T(1,128)}), f32[16,1,36864]{2,1,0:T(1,128)S(1)}, u32[]{:S(2)}, u32[]{:S(2)}) async-start(f32[16,1,36864]{2,1,0:T(1,128)} %reshape.75), calls=%async_computation | async-start | bytes 4718592 | tf_op jit(solution)/shard_map/all_to_all | solution.py:68
  46.1 0.1 broadcast_add_fusion
  46.1 0.1 broadcast_in_dim.2
  46.2 0.1 broadcast_in_dim_reshape.2
  46.3 31.0 %all-to-all-done = f32[16,1,36864]{2,1,0:T(1,128)S(1)} async-done(((f32[16,1,36864]{2,1,0:T(1,128)}), f32[16,1,36864]{2,1,0:T(1,128)S(1)}, u32[]{:S(2)}, u32[]{:S(2)}) %all-to-all-start) | async-done | bytes 2359328 | tf_op jit(solution)/shard_map/all_to_all | solution.py:68
  77.3 1.4 copy-done.4
  78.7 0.6 broadcast.95
  79.3 8.0 %reduce = f32[16,36864]{1,0:T(8,128)S(1)} reduce(f32[16,1,36864]{2,1,0:T(1,128)} %copy-done.4, f32[]{:T(128)} %broadcast.95), dimensions={1}, to_apply=%all_to_all.26.reduce_sub_computation | reduce | bytes 4718596 | tf_op jit(solution)/shard_map/all_to_all | solution.py:68
  87.3 21.2 %reshape.76 = f32[4096,9,16]{2,1,0:T(8,128)} reshape(f32[16,36864]{1,0:T(8,128)S(1)} %reduce) | data formatting | bytes 4718592
  108.5 18.9 %copy.70 = f32[9,16,16,256]{3,2,1,0:T(8,128)S(1)} copy(f32[9,16,16,256]{2,0,3,1:T(8,128)} %bitcast.112) | data formatting | bytes 4718592 | tf_op jit(solution)/shard_map/all_to_all | solution.py:68
  127.4 0.0 copy-start.7
  127.4 1.5 copy.71
  128.9 3.3 fusion.13
  132.2 2.4 fusion.89
  134.6 0.7 collective-permute-start
  135.3 2.8 collective-permute-start.1
  138.1 0.7 fusion.90
  145.0 23.4 %collective-permute-done = bf16[6,256,256]{2,1,0:T(8,128)(2,1)} collective-permute-done((bf16[6,256,256]{2,1,0:T(8,128)(2,1)}, bf16[6,256,256]{2,1,0:T(8,128)(2,1)}, u32[]{:S(2)}, u32[]{:S(2)}) %collective-permute-start) | collective-permute-done | bytes 786464 | tf_op jit(solution)/shard_map/ppermute | solution.py:21
  168.4 2.3 collective-permute-done.1
  170.7 2.2 pad_maximum_fusion
  172.9 0.0 slice-start.1
  172.9 1.9 fusion.21
  174.8 1.8 fusion.25
  176.5 0.0 slice-done
  176.5 0.0 slice-done.1
  176.6 0.5 fusion.29
  177.0 0.0 copy-start.1
  177.0 0.5 fusion.17
  177.5 0.8 copy-done.1
  178.3 2.7 multiply_reduce_fusion.2
  181.0 0.1 reshape.69
  181.1 0.1 reshape.70
  181.2 15.0 %all-reduce.3 = (f32[32]{0:T(128)S(1)}, f32[32]{0:T(128)S(1)}) all-reduce(f32[32]{0:T(128)S(1)} %reduce_sum.73, f32[32]{0:T(128)S(1)} %reduce_sum.75), channel_id=1, replica_groups=mesh['sx'=8,'sz'=16] {'sx'}, use_global_device_ids=true, to_apply=%region_2.3 | all-reduce | flops 64 | bytes 512 | tf_op jit(solution)/shard_map/psum | solution.py:62
  196.2 38.0 %all-reduce.1 = (f32[32]{0:T(128)S(1)}, f32[32]{0:T(128)S(1)}) all-reduce(f32[32]{0:T(128)S(1)} %get-tuple-element.15, f32[32]{0:T(128)S(1)} %get-tuple-element.16), channel_id=1, replica_groups=mesh['sx'=8,'sz'=16] {'sz'}, use_global_device_ids=true, to_apply=%region_3.4 | all-reduce | flops 64 | bytes 512 | tf_op jit(solution)/shard_map/psum | solution.py:62
  234.2 0.1 mul.87
  234.2 3.8 fusion.14
  238.0 1.6 fusion.88
  239.7 0.1 collective-permute-start.2
  239.7 0.0 slice-start.3
  239.8 3.6 collective-permute-start.3
  243.3 29.8 %collective-permute-done.2 = bf16[6,256,256]{2,1,0:T(8,128)(2,1)S(1)} collective-permute-done((bf16[6,256,256]{2,1,0:T(8,128)(2,1)S(1)}, bf16[6,256,256]{2,1,0:T(8,128)(2,1)S(1)}, u32[]{:S(2)}, u32[]{:S(2)}) %collective-permute-start.2) | collective-permute-done | bytes 786464 | tf_op jit(solution)/shard_map/ppermute | solution.py:21
  273.1 2.0 collective-permute-done.3
  275.1 1.6 pad_maximum_fusion.1
  276.7 1.8 fusion.23
  278.5 0.5 fusion.27
  279.0 0.5 fusion.31
  279.5 0.0 copy-start.3
  279.5 0.5 fusion.19
  280.0 0.8 copy-done.2
  280.7 0.8 copy-done.3
  281.5 1.5 multiply_reduce_fusion
  283.0 0.1 reshape.71
  283.1 0.1 reshape.72
  283.2 12.7 %all-reduce.2 = (f32[32]{0:T(128)S(1)}, f32[32]{0:T(128)S(1)}) all-reduce(f32[32]{0:T(128)S(1)} %reduce_sum.77, f32[32]{0:T(128)S(1)} %reduce_sum.79), channel_id=1, replica_groups=mesh['sx'=8,'sz'=16] {'sx'}, use_global_device_ids=true, to_apply=%region_10.11 | all-reduce | flops 64 | bytes 512 | tf_op jit(solution)/shard_map/psum | solution.py:62
  295.9 37.5 %all-reduce = (f32[32]{0:T(128)S(1)}, f32[32]{0:T(128)S(1)}) all-reduce(f32[32]{0:T(128)S(1)} %get-tuple-element.13, f32[32]{0:T(128)S(1)} %get-tuple-element.14), channel_id=1, replica_groups=mesh['sx'=8,'sz'=16] {'sz'}, use_global_device_ids=true, to_apply=%region_11.12 | all-reduce | flops 64 | bytes 512 | tf_op jit(solution)/shard_map/psum | solution.py:62
  333.4 0.1 mul.95
  333.5 2.0 fusion.5
  335.5 1.5 copy.80
  337.0 53.9 %all_to_all.36 = f32[9,256,256]{2,0,1:T(8,128)S(1)} all-to-all(f32[9,256,256]{2,0,1:T(8,128)S(1)} %copy.80), channel_id=1, replica_groups=mesh['sx'=8,'sz'=16] {'sz'}, dimensions={1} | all-to-all | bytes 4718592 | tf_op jit(solution)/shard_map/all_to_all | solution.py:75
  390.8 1.4 copy.81
  392.2 1.6 all_to_all.33
  (25 shorter events, 0.2 us)
Async XLA Ops:
  0.0 128.9 %copy-start = (bf16[256,256]{1,0:T(8,128)(2,1)S(1)}, bf16[256,256]{1,0:T(8,128)(2,1)}, u32[]{:S(2)}) copy-start(bf16[256,256]{1,0:T(8,128)(2,1)} %param.9) | copy-start | bytes 393220
  36.9 40.4 %all-to-all-start = ((f32[16,1,36864]{2,1,0:T(1,128)}), f32[16,1,36864]{2,1,0:T(1,128)S(1)}, u32[]{:S(2)}, u32[]{:S(2)}) async-start(f32[16,1,36864]{2,1,0:T(1,128)} %reshape.75), calls=%async_computation | async-start | bytes 4718592 | tf_op jit(solution)/shard_map/all_to_all | solution.py:68
  77.3 1.4 copy-start.4
  127.4 1.5 copy-start.6
  127.4 1.5 copy-start.7
  132.2 5.9 %copy-start.5 = (s32[5]{0:T(128)S(1)}, s32[5]{0:T(128)}, u32[]{:S(2)}) copy-start(s32[5]{0:T(128)} %param.8) | copy-start | bytes 64
  134.6 33.8 %collective-permute-start = (bf16[6,256,256]{2,1,0:T(8,128)(2,1)}, bf16[6,256,256]{2,1,0:T(8,128)(2,1)}, u32[]{:S(2)}, u32[]{:S(2)}) collective-permute-start(bf16[6,256,256]{2,1,0:T(8,128)(2,1)} %get-tuple-element.19), channel_id=1, source_target_pairs={{0,16},{16,32},{32,48},{48,64},{64,80},{80,96},{96,112},{112,0},{1... | collective-permute-start | bytes 2359304 | tf_op jit(solution)/shard_map/ppermute | solution.py:21
  135.3 35.4 %collective-permute-start.1 = (bf16[6,256,256]{2,1,0:T(8,128)(2,1)S(1)}, bf16[6,256,256]{2,1,0:T(8,128)(2,1)}, u32[]{:S(2)}, u32[]{:S(2)}) collective-permute-start(bf16[6,256,256]{2,1,0:T(8,128)(2,1)S(1)} %get-tuple-element.20), channel_id=1, source_target_pairs={{16,0},{32,16},{48,32},{64,48},{80,64},{96,80},{112,96},{0,112},{1... | collective-permute-start | bytes 2359304 | tf_op jit(solution)/shard_map/ppermute | solution.py:22
  170.7 5.9 %slice-start = ((s8[5898240]{0:T(1024)(128)(4,1)}), s8[4194304]{0:T(1024)(128)(4,1)S(1)}, s32[]{:S(2)}) async-start(s8[5898240]{0:T(1024)(128)(4,1)} %bitcast.116), calls=%async_computation.2 | async-start | bytes 8388608
  172.9 3.7 slice-start.1
  177.0 1.3 copy-start.1
  238.0 40.4 %slice-start.2 = ((s8[5898240]{0:T(1024)(128)(4,1)}), s8[4194304]{0:T(1024)(128)(4,1)S(1)}, s32[]{:S(2)}) async-start(s8[5898240]{0:T(1024)(128)(4,1)} %bitcast.118), calls=%async_computation.4 | async-start | bytes 8388608
  239.7 33.5 %collective-permute-start.2 = (bf16[6,256,256]{2,1,0:T(8,128)(2,1)S(1)}, bf16[6,256,256]{2,1,0:T(8,128)(2,1)S(1)}, u32[]{:S(2)}, u32[]{:S(2)}) collective-permute-start(bf16[6,256,256]{2,1,0:T(8,128)(2,1)S(1)} %get-tuple-element.17), channel_id=1, source_target_pairs={{0,16},{16,32},{32,48},{48,64},{64,80},{80,96},{96,112},{112,0},{1... | collective-permute-start | bytes 2359304 | tf_op jit(solution)/shard_map/ppermute | solution.py:21
  239.7 38.7 %slice-start.3 = ((s8[5898240]{0:T(1024)(128)(4,1)}), s8[1703936]{0:T(1024)(128)(4,1)S(1)}, s32[]{:S(2)}) async-start(s8[5898240]{0:T(1024)(128)(4,1)} %bitcast.118), calls=%async_computation.5 | async-start | bytes 3407872
  239.8 35.4 %collective-permute-start.3 = (bf16[6,256,256]{2,1,0:T(8,128)(2,1)S(1)}, bf16[6,256,256]{2,1,0:T(8,128)(2,1)S(1)}, u32[]{:S(2)}, u32[]{:S(2)}) collective-permute-start(bf16[6,256,256]{2,1,0:T(8,128)(2,1)S(1)} %get-tuple-element.18), channel_id=1, source_target_pairs={{16,0},{32,16},{48,32},{64,48},{80,64},{96,80},{112,96},{0,112},{1... | collective-permute-start | bytes 2359304 | tf_op jit(solution)/shard_map/ppermute | solution.py:22
  279.5 1.3 copy-start.2
  279.5 2.0 copy-start.3
